TPU v7x, 32 devices: a whole 2x2x4 slice. The times are simulated.
32 devices in a mesh: seq: 8 (over y, x, core), head: 4 (over z).
Axes of the slice: x: 2, y: 2, z: 4, core: 2. Of those that a mesh axis runs over, the one named last changes fastest.
Arguments:
- dna: bfloat16 [6144, 768], P('seq')
- conv_in: bfloat16 [5, 1536, 768], P(None, 'head')
- dilated_kernel_weight: bfloat16 [3, 1536, 1536], P(None, 'head'), may hold values from -0.09375 to 0.09375
- w_query: bfloat16 [1536, 1536], P('head')
- w_key: bfloat16 [1536, 1536], P('head')
- w_value: bfloat16 [1536, 1536], P('head'), may hold values from -0.15625 to 0.15625
- w_out: bfloat16 [1536, 1536], P('head'), may hold values from -0.21875 to 0.21875
Outputs:
- encoded: bfloat16 [3072, 1536], P('seq', 'head')
All inputs are finite; a program needn't handle non-finite values.
Results may differ from a plain program's by a relative error of at most 0.007.
Values may be sent and summed in bfloat16 or wider, within the bound.
No kernel may reach another device: no remote copies, remote signals or barrier semaphores. Data moves between devices by JAX's collectives and lax.ppermute only.
A program may use at most 64 MiB of HBM per device.

v0:
```python
import math
import jax
import jax.numpy as jnp
from jax import lax
from jax.sharding import PartitionSpec as P

C = 1536
HEAD_DIM = 64
KW = 5
DILATION_STEP = 4


def padded_2(block, sides, width):
    for axis, dim in sides:
        count = lax.axis_size(axis)
        forward = [(i, i + 1) for i in range(count - 1)]
        backward = [(target, source) for source, target in forward]
        low = lax.ppermute(
            lax.slice_in_dim(block, block.shape[dim] - width, None, axis=dim), axis, forward
        )
        high = lax.ppermute(lax.slice_in_dim(block, 0, width, axis=dim), axis, backward)
        block = jnp.concatenate([low, block, high], axis=dim)
    return block


def row_scale(hidden):
    squares = lax.psum(jnp.sum(hidden * hidden, axis=1), "head")
    return hidden * lax.rsqrt(squares / C + 1e-06)[:, None]


def reduce_operands(left, right):
    return lax.dot_general(
        left, right, (((1,), (1,)), ((), ())), preferred_element_type=jnp.float32
    )


def on_device(dna, conv_in, dilated_kernel_weight, w_query, w_key, w_value, w_out):
    local_row_count = dna.shape[0] // 2
    half = (KW - 1) // 2
    padded = padded_2(dna, (("seq", 0),), half)
    h1 = jnp.zeros((local_row_count, conv_in.shape[1]), jnp.float32)
    for kernel_offset in range(KW):
        rows = lax.slice(
            padded,
            (kernel_offset, 0),
            (kernel_offset + 2 * local_row_count - 1, padded.shape[1]),
            (2, 1),
        )
        h1 = h1 + reduce_operands(rows, conv_in[kernel_offset])
    gelu_output = jax.nn.gelu(row_scale(h1), approximate=True).astype(jnp.bfloat16)
    complete_output = lax.all_gather(gelu_output, "head", axis=1, tiled=True)
    broad_input = padded_2(complete_output, (("seq", 0),), DILATION_STEP)
    second_hidden = h1
    for kernel_offset in range(3):
        second_hidden = second_hidden + reduce_operands(
            broad_input[
                DILATION_STEP * kernel_offset : DILATION_STEP * kernel_offset + local_row_count
            ],
            dilated_kernel_weight[kernel_offset],
        )
    normed = row_scale(second_hidden).astype(jnp.bfloat16)
    local_width = w_query.shape[0]
    heads_here = local_width // HEAD_DIM
    empty = jnp.zeros((local_row_count, local_width), jnp.float32)
    totals = (empty, empty, empty)
    piece = lax.all_gather(normed, "head", axis=1, tiled=True)
    count = piece.shape[1]
    outs = []
    for total, weight in zip(totals, (w_query, w_key, w_value)):
        block = lax.slice_in_dim(weight, 0, count, axis=1)
        outs.append(total + reduce_operands(piece, block))
    q_acc, k_acc, v_acc = tuple(outs)
    query = q_acc.astype(jnp.bfloat16).reshape(local_row_count, heads_here, HEAD_DIM)
    keys = k_acc.astype(jnp.bfloat16)
    values = v_acc.astype(jnp.bfloat16)
    scale = 1.0 / math.sqrt(HEAD_DIM)
    start_state = (
        jnp.full((heads_here, local_row_count), -1e30, jnp.float32),
        jnp.zeros((heads_here, local_row_count), jnp.float32),
        jnp.zeros((local_row_count, heads_here, HEAD_DIM), jnp.float32),
    )
    key_rows = lax.all_gather(keys, "seq", axis=0, tiled=True)
    value_rows = lax.all_gather(values, "seq", axis=0, tiled=True)
    count = key_rows.shape[0]
    width = 512 if count % 512 == 0 else count
    blocks = count // width
    key_blocks = key_rows.reshape(blocks, width, heads_here, HEAD_DIM)
    value_blocks = value_rows.reshape(blocks, width, heads_here, HEAD_DIM)

    def step(state, operands):
        running, total, acc = state
        key_block, value_block = operands
        scores = (
            jnp.einsum("qhd,khd->hqk", query, key_block, preferred_element_type=jnp.float32) * scale
        )
        newest = jnp.maximum(running, jnp.max(scores, axis=2))
        factor = jnp.exp(running - newest)
        weights = jnp.exp(scores - newest[:, :, None])
        total = total * factor + jnp.sum(weights, axis=2)
        update = jnp.einsum(
            "hqk,khd->qhd",
            weights.astype(jnp.bfloat16),
            value_block,
            preferred_element_type=jnp.float32,
        )
        acc = acc * jnp.transpose(factor)[:, :, None] + update
        return ((newest, total, acc), None)

    state, _ = lax.scan(step, start_state, (key_blocks, value_blocks))
    running, total, acc = state
    attended = (
        (acc / jnp.transpose(total)[:, :, None])
        .reshape(local_row_count, local_width)
        .astype(jnp.bfloat16)
    )
    partial_out = jnp.dot(attended, w_out, preferred_element_type=jnp.float32)
    mixed = lax.psum_scatter(
        partial_out.astype(jnp.bfloat16), "head", scatter_dimension=1, tiled=True
    ).astype(jnp.float32)
    return (second_hidden + mixed).astype(jnp.bfloat16)


def solution(mesh):
    in_specs = (
        P("seq", None),
        P(None, "head", None),
        P(None, "head", None),
        P("head", None),
        P("head", None),
        P("head", None),
        P("head", None),
    )
    out_specs = P("seq", "head")
    return jax.shard_map(
        on_device, mesh=mesh, in_specs=in_specs, out_specs=out_specs, check_vma=False
    )
```

profile of v0, /device:TPU:0, one launch (start us, length us, event | category | flops | bytes accessed | tf_op | source)
XLA Modules:
  0.0 285.1 jit_solution(8050887976854538106)
XLA Ops:
  7.4 2.3 collective-permute-start
  11.1 5.0 %slice.65 = bf16[384,768]{1,0:T(8,128)(2,1)S(1)} slice(bf16[768,768]{1,0:T(8,128)(2,1)} %param.9), slice={[0:767:2], [0:768:1]} | slice | bytes 1179648 | tf_op jit(solution)/shard_map/slice | solution.py:43
  16.1 2.4 fusion.44
  18.5 3.5 %slice.67 = bf16[384,768]{1,0:T(8,128)(2,1)} slice(bf16[768,768]{1,0:T(8,128)(2,1)S(1)} %copy-done.1), slice={[1:768:2], [0:768:1]} | slice | bytes 1179648 | tf_op jit(solution)/shard_map/slice | solution.py:43
  23.0 3.7 %slice.69 = bf16[384,768]{1,0:T(8,128)(2,1)} slice(bf16[772,768]{1,0:T(8,128)(2,1)S(1)} %pad_maximum_fusion), slice={[4:771:2], [0:768:1]} | slice | bytes 1179648 | tf_op jit(solution)/shard_map/slice | solution.py:43
  27.8 3.6 %slice.61 = bf16[384,768]{1,0:T(8,128)(2,1)} slice(bf16[772,768]{1,0:T(8,128)(2,1)S(1)} %pad_maximum_fusion), slice={[0:767:2], [0:768:1]} | slice | bytes 1179648 | tf_op jit(solution)/shard_map/slice | solution.py:43
  38.0 12.8 %psum.14 = f32[384]{0:T(512)S(1)} all-reduce(f32[384]{0:T(512)S(1)} %get-tuple-element.105), channel_id=1, replica_groups=mesh['seq'=8,'head'=4] {'head'}, use_global_device_ids=true, to_apply=%region_1.0 | all-reduce | flops 384 | bytes 3072 | tf_op jit(solution)/shard_map/psum | solution.py:27
  51.8 31.3 %all-gather.5.cloned.1.call-done = bf16[384,1536]{0,1:T(8,128)(2,1)} async-done(((bf16[384,384]{0,1:T(8,128)(2,1)}), bf16[384,1536]{0,1:T(8,128)(2,1)}) %all-gather.5.cloned.1.call-update) | async-done | bytes 1179664 | tf_op jit(solution)/shard_map/all_gather | solution.py:51
  86.0 3.1 %collective-permute-start.2 = (bf16[4,1536]{0,1:T(8,128)(2,1)S(1)}, bf16[4,1536]{0,1:T(8,128)(2,1)S(1)}, u32[]{:S(2)}, u32[]{:S(2)}) collective-permute-start(bf16[4,1536]{0,1:T(8,128)(2,1)S(1)} %get-tuple-element.102), channel_id=1, source_target_pairs={{0,4},{4,8},{8,12},{12,16},{16,20},{20,24},{24,28},{1,5},{5,9},{9,... | collective-permute-start | bytes 36872 | tf_op jit(solution)/shard_map/ppermute | solution.py:18
  89.1 2.4 fusion.28
  93.3 9.9 %psum.15 = f32[384]{0:T(512)S(1)} all-reduce(f32[384]{0:T(512)S(1)} %get-tuple-element.107), channel_id=1, replica_groups=mesh['seq'=8,'head'=4] {'head'}, use_global_device_ids=true, to_apply=%region_3.0 | all-reduce | flops 384 | bytes 3072 | tf_op jit(solution)/shard_map/psum | solution.py:27
  104.1 35.4 %all-gather.7.cloned.1.call-done = bf16[384,1536]{0,1:T(8,128)(2,1)} async-done(((bf16[384,384]{0,1:T(8,128)(2,1)}), bf16[384,1536]{0,1:T(8,128)(2,1)}) %all-gather.7.cloned.1.call-update) | async-done | bytes 1179664 | tf_op jit(solution)/shard_map/all_gather | solution.py:66
  139.4 3.2 %convolution_convert_fusion.3 = bf16[384,384]{1,0:T(8,128)(2,1)} fusion(bf16[384,1536]{0,1:T(8,128)(2,1)} %all-gather.7.cloned.1.call-done, bf16[384,1536]{1,0:T(8,128)(2,1)} %param.13), kind=kOutput, calls=%fused_computation.34 | convolution fusion | flops 453132288 | bytes 2654208 | tf_op jit(solution)/shard_map/dot_general | solution.py:32
  142.7 3.2 %convolution_convert_fusion.2 = bf16[384,384]{1,0:T(8,128)(2,1)} fusion(bf16[384,1536]{0,1:T(8,128)(2,1)} %all-gather.7.cloned.1.call-done, bf16[384,1536]{1,0:T(8,128)(2,1)} %param.14), kind=kOutput, calls=%fused_computation.33 | convolution fusion | flops 453132288 | bytes 2654208 | tf_op jit(solution)/shard_map/dot_general | solution.py:32
  146.1 2.4 convolution_convert_fusion.1
  148.5 22.4 %all-gather.9.cloned.1.call-done = bf16[3072,384]{1,0:T(8,128)(2,1)} async-done(((bf16[384,384]{1,0:T(8,128)(2,1)}), bf16[3072,384]{1,0:T(8,128)(2,1)}) %all-gather.9.cloned.1.call-update) | async-done | bytes 2359312 | tf_op jit(solution)/shard_map/all_gather | solution.py:82
  170.9 8.1 %reshape.19 = bf16[6,512,6,64]{3,2,1,0:T(8,128)(2,1)} reshape(bf16[3072,384]{1,0:T(8,128)(2,1)} %all-gather.9.cloned.1.call-done) | data formatting | bytes 4718592 | tf_op jit(solution)/shard_map/reshape | solution.py:87
  179.0 7.2 %copy.16 = bf16[6,512,6,64]{1,3,2,0:T(8,128)(2,1)} copy(bf16[6,512,6,64]{3,2,1,0:T(8,128)(2,1)} %reshape.19) | data formatting | bytes 4718592
  186.2 15.4 %all-gather.11.cloned.1.call-done = bf16[3072,384]{1,0:T(8,128)(2,1)} async-done(((bf16[384,384]{1,0:T(8,128)(2,1)}), bf16[3072,384]{1,0:T(8,128)(2,1)}) %all-gather.11.cloned.1.call-update) | async-done | bytes 2359312 | tf_op jit(solution)/shard_map/all_gather | solution.py:83
  201.7 8.1 %reshape.20 = bf16[6,512,6,64]{3,2,1,0:T(8,128)(2,1)} reshape(bf16[3072,384]{1,0:T(8,128)(2,1)} %all-gather.11.cloned.1.call-done) | data formatting | bytes 4718592 | tf_op jit(solution)/shard_map/reshape | solution.py:88
  209.8 7.1 %copy.17 = bf16[6,512,6,64]{1,3,2,0:T(8,128)(2,1)} copy(bf16[6,512,6,64]{3,2,1,0:T(8,128)(2,1)} %reshape.20) | data formatting | bytes 4718592
  216.9 28.4 %while.15 = (s32[]{:T(128)}, f32[6,384]{1,0:T(8,128)S(1)}, f32[6,384]{1,0:T(8,128)S(1)}, f32[384,6,64]{0,2,1:T(8,128)S(1)}, bf16[6,512,6,64]{1,3,2,0:T(8,128)(2,...) while((s32[]{:T(128)}, f32[6,384]{1,0:T(8,128)S(1)}, ...), condition=%wide.region_7.8_spmd.clone, body=%wide.region_4.7_spmd.clone.sunk | while | flops 311883264 | bytes 16564345 | solution.py:109
  219.6 2.0 fusion.86
  247.4 29.3 %reduce-scatter.2.cloned.1.call-done = bf16[384,384]{0,1:T(8,128)(2,1)} async-done(((bf16[384,1536]{0,1:T(8,128)(2,1)}), bf16[384,384]{0,1:T(8,128)(2,1)}) %reduce-scatter.2.cloned.1.call-update) | async-done | bytes 294928 | tf_op jit(solution)/shard_map/reduce_scatter | solution.py:117
  (86 shorter events, 47.6 us)
Async XLA Ops:
  6.5 238.8 %copy-start = (bf16[384,1536]{1,0:T(8,128)(2,1)S(1)}, bf16[384,1536]{1,0:T(8,128)(2,1)}, u32[]{:S(2)}) copy-start(bf16[384,1536]{1,0:T(8,128)(2,1)} %param.15) | copy-start | bytes 3538948
  6.5 12.0 %copy-start.1 = (bf16[768,768]{1,0:T(8,128)(2,1)S(1)}, bf16[768,768]{1,0:T(8,128)(2,1)}, u32[]{:S(2)}) copy-start(bf16[768,768]{1,0:T(8,128)(2,1)} %param.9) | copy-start | bytes 3538948
  6.5 76.6 %all-gather.5.cloned.1.call-start = ((), (), s32[]{:S(2)}) async-start(), calls=%async_computation.1 | async-start | bytes 1474560 | tf_op jit(solution)/shard_map/all_gather | solution.py:51
  7.4 14.6 %collective-permute-start = (bf16[2,768]{1,0:T(2,128)(2,1)S(1)}, bf16[2,768]{1,0:T(2,128)(2,1)S(1)}, u32[]{:S(2)}, u32[]{:S(2)}) collective-permute-start(bf16[2,768]{1,0:T(2,128)(2,1)S(1)} %get-tuple-element.103), channel_id=1, source_target_pairs={{0,4},{4,8},{8,12},{12,16},{16,20},{20,24},{24,28},{1,5},{5,9},{9,... | collective-permute-start | bytes 9224 | tf_op jit(solution)/shard_map/ppermute | solution.py:18
  9.8 12.3 %collective-permute-start.1 = (bf16[2,768]{1,0:T(2,128)(2,1)S(1)}, bf16[2,768]{1,0:T(2,128)(2,1)}, u32[]{:S(2)}, u32[]{:S(2)}) collective-permute-start(bf16[2,768]{1,0:T(2,128)(2,1)S(1)} %get-tuple-element.104), channel_id=1, source_target_pairs={{4,0},{8,4},{12,8},{16,12},{20,16},{24,20},{28,24},{5,1},{9,5},{13... | collective-permute-start | bytes 9224 | tf_op jit(solution)/shard_map/ppermute | solution.py:21
  26.7 6.3 %copy-start.2 = (f32[384,384]{0,1:T(8,128)S(1)}, f32[384,384]{0,1:T(8,128)}, u32[]{:S(2)}) copy-start(f32[384,384]{0,1:T(8,128)} %fusion.44) | copy-start | bytes 1769476
  31.4 3.5 %copy-start.3 = (bf16[384,768]{1,0:T(8,128)(2,1)S(1)}, bf16[384,768]{1,0:T(8,128)(2,1)}, u32[]{:S(2)}) copy-start(bf16[384,768]{1,0:T(8,128)(2,1)} %slice.67) | copy-start | bytes 1769476
  33.0 3.4 %copy-start.4 = (bf16[384,768]{1,0:T(8,128)(2,1)S(1)}, bf16[384,768]{1,0:T(8,128)(2,1)}, u32[]{:S(2)}) copy-start(bf16[384,768]{1,0:T(8,128)(2,1)} %slice.69) | copy-start | bytes 1769476
  51.8 87.7 %all-gather.7.cloned.1.call-start = ((), (), s32[]{:S(2)}) async-start(), calls=%async_computation.2 | async-start | bytes 1474560 | tf_op jit(solution)/shard_map/all_gather | solution.py:66
  83.1 8.4 %copy-start.5 = (bf16[384,1536]{0,1:T(8,128)(2,1)S(1)}, bf16[384,1536]{0,1:T(8,128)(2,1)}, u32[]{:S(2)}) copy-start(bf16[384,1536]{0,1:T(8,128)(2,1)} %all-gather.5.cloned.1.call-done) | copy-start | bytes 3538948
  83.1 8.4 %copy-start.6 = (bf16[3,384,1536]{2,1,0:T(8,128)(2,1)S(1)}, bf16[3,384,1536]{2,1,0:T(8,128)(2,1)}, u32[]{:S(2)}) copy-start(bf16[3,384,1536]{2,1,0:T(8,128)(2,1)} %param.11) | copy-start | bytes 10616836
  84.6 7.8 %collective-permute-start.3 = (bf16[4,1536]{0,1:T(8,128)(2,1)S(1)}, bf16[4,1536]{0,1:T(8,128)(2,1)S(1)}, u32[]{:S(2)}, u32[]{:S(2)}) collective-permute-start(bf16[4,1536]{0,1:T(8,128)(2,1)S(1)} %get-tuple-element.101), channel_id=1, source_target_pairs={{4,0},{8,4},{12,8},{16,12},{20,16},{24,20},{28,24},{5,1},{9,5},{13... | collective-permute-start | bytes 36872 | tf_op jit(solution)/shard_map/ppermute | solution.py:21
  86.0 5.5 %collective-permute-start.2 = (bf16[4,1536]{0,1:T(8,128)(2,1)S(1)}, bf16[4,1536]{0,1:T(8,128)(2,1)S(1)}, u32[]{:S(2)}, u32[]{:S(2)}) collective-permute-start(bf16[4,1536]{0,1:T(8,128)(2,1)S(1)} %get-tuple-element.102), channel_id=1, source_target_pairs={{0,4},{4,8},{8,12},{12,16},{16,20},{20,24},{24,28},{1,5},{5,9},{9,... | collective-permute-start | bytes 36872 | tf_op jit(solution)/shard_map/ppermute | solution.py:18
  104.0 66.9 %all-gather.9.cloned.1.call-start = ((), (), s32[]{:S(2)}) async-start(), calls=%async_computation.3 | async-start | bytes 2654208 | tf_op jit(solution)/shard_map/all_gather | solution.py:82
  142.6 59.1 %all-gather.11.cloned.1.call-start = ((), (), s32[]{:S(2)}) async-start(), calls=%async_computation.4 | async-start | bytes 2654208 | tf_op jit(solution)/shard_map/all_gather | solution.py:83
  145.9 130.8 %reduce-scatter.2.cloned.1.call-start = ((), (), s32[]{:S(2)}) async-start(), calls=%async_computation.5 | async-start | bytes 1474560 | tf_op jit(solution)/shard_map/reduce_scatter | solution.py:117
Sparse Core Ops, SparseCore 0:
  51.9 31.1 all-gather.4
  104.1 35.2 all-gather.6
  142.7 28.1 all-gather.8
  172.6 29.0 all-gather.10
  247.5 29.1 reduce-scatter.1
where the time goes:
time: 287 us; the launch traced here: 285 us
  waiting for transfers between devices  134 us (47%)
  local copies, waits for them, and re-layouts  50.8 us (18%)
  matrix products  47 us (16%)
  blocking collectives  22.7 us (8%)
  between operations  13.4 us (5%)
  other arithmetic  8.58 us (3%)
  starting transfers between devices  8.47 us (3%)
    all_gather x1, waiting for transfers between devices, on_device(): piece = lax.all_gather(normed, 'head', axis=1, tiled=True)  35.4 us
    all_gather x1, waiting for transfers between devices, on_device(): complete_output = lax.all_gather(gelu_output, 'head', axis=1, tiled=True)  31.3 us
    reduce_scatter x1, waiting for transfers between devices, on_device(): lax.psum_scatter(partial_out.astype(jnp.bfloat16), 'head', scatter_dimens...  29.3 us
    psum x2, blocking collectives, row_scale(): squares = lax.psum(jnp.sum(hidden * hidden, axis=1), 'head')  22.7 us
    all_gather x1, waiting for transfers between devices, on_device(): key_rows = lax.all_gather(keys, 'seq', axis=0, tiled=True)  22.4 us
    dot_general x11, matrix products, reduce_operands(): lax.dot_general(left, right, (((1,), (1,)), ((), ())), preferred_element_...  21.8 us
    slice x5, local copies, waits for them, and re-layouts, on_device(): lax.slice(padded, (kernel_offset, 0), (kernel_offset + 2 * local_row_coun...  17 us
    all_gather x1, waiting for transfers between devices, on_device(): value_rows = lax.all_gather(values, 'seq', axis=0, tiled=True)  15.4 us
  transfers between devices with their start and end apart: 9, of which 5 were waited for; matrix products, arithmetic and copies ran while one was open for 12% of the time, Pallas kernels for 0%

commit v1 on v0

--- a/solution.py
+++ b/solution.py
@@ -79,7 +79,16 @@
         jnp.zeros((heads_here, local_row_count), jnp.float32),
         jnp.zeros((local_row_count, heads_here, HEAD_DIM), jnp.float32),
     )
-    key_rows = lax.all_gather(keys, "seq", axis=0, tiled=True)
+    ways = lax.axis_size("seq")
+    up = [(d, (d + 1) % ways) for d in range(ways)]
+    down = [(d, (d - 1) % ways) for d in range(ways)]
+    earlier, later = ([keys], [keys])
+    for __2 in range(ways // 2):
+        earlier.append(lax.ppermute(earlier[-1], "seq", up))
+    for __2 in range((ways - 1) // 2):
+        later.append(lax.ppermute(later[-1], "seq", down))
+    line = jnp.concatenate([*earlier[::-1], *later[1:]], axis=0)
+    key_rows = jnp.roll(line, (lax.axis_index("seq") - ways // 2) * keys.shape[0], axis=0)
     value_rows = lax.all_gather(values, "seq", axis=0, tiled=True)
     count = key_rows.shape[0]
     width = 512 if count % 512 == 0 else count

time: 287 us -> 320 us (1.11)
  matrix products: 47 us -> 68.6 us
  local copies, waits for them, and re-layouts: 50.8 us -> 63.2 us
  waiting for transfers between devices: 134 us -> 127 us
  starting transfers between devices: 8.47 us -> 14 us
    ppermute x0 -> x7, waiting for transfers between devices: none -> 31.3 us  [the longest x4 31.3 us: on_device(): earlier.append(lax.ppermute(earlier[-1], 'seq', up))]
    all_gather x1 -> x0, waiting for transfers between devices: 22.4 us -> none  [on_device(): key_rows = lax.all_gather(keys, 'seq', axis=0, tiled=True)]
    all_gather x1, waiting for transfers between devices: 15.4 us -> 0.01 us  [on_device(): value_rows = lax.all_gather(values, 'seq', axis=0, tiled=True)]
    dot_general x6, matrix products: 11 us -> 23.7 us  [step(): jnp.einsum('qhd,khd->hqk', query, key_block, preferred_element_type=jnp.f...]
    dot_general x6, matrix products: 12.2 us -> 21.8 us  [step(): jnp.einsum('hqk,khd->qhd', weights.astype(jnp.bfloat16), value_block, pre...]
    unnamed x16 -> x35, local copies, waits for them, and re-layouts: 14.4 us -> 23.4 us
    ppermute x0 -> x7, starting transfers between devices: none -> 7.51 us  [the longest x3 7.44 us: on_device(): later.append(lax.ppermute(later[-1], 'seq', down))]
  transfers between devices with their start and end apart: 9 -> 15, of which waited for: 5 -> 8; matrix products, arithmetic and copies ran while one was open for 12% -> 14% of each run, Pallas kernels for 0% -> 0%
where the time goes in v1:
time: 320 us; the launch traced here: 318 us
  waiting for transfers between devices  127 us (40%)
  matrix products  68.6 us (21%)
  local copies, waits for them, and re-layouts  63.2 us (20%)
  blocking collectives  22.7 us (7%)
  starting transfers between devices  14 us (4%)
  between operations  13.5 us (4%)
  other arithmetic  8.56 us (3%)
    all_gather x1, waiting for transfers between devices, on_device(): piece = lax.all_gather(normed, 'head', axis=1, tiled=True)  33.5 us
    ppermute x4, waiting for transfers between devices, on_device(): earlier.append(lax.ppermute(earlier[-1], 'seq', up))  31.3 us
    all_gather x1, waiting for transfers between devices, on_device(): complete_output = lax.all_gather(gelu_output, 'head', axis=1, tiled=True)  31.3 us
    reduce_scatter x1, waiting for transfers between devices, on_device(): lax.psum_scatter(partial_out.astype(jnp.bfloat16), 'head', scatter_dimens...  30.1 us
    dot_general x6, matrix products, step(): jnp.einsum('qhd,khd->hqk', query, key_block, preferred_element_type=jnp.f...  23.7 us
    unnamed x35, local copies, waits for them, and re-layouts  23.4 us
    psum x2, blocking collectives, row_scale(): squares = lax.psum(jnp.sum(hidden * hidden, axis=1), 'head')  22.7 us
    dot_general x6, matrix products, step(): jnp.einsum('hqk,khd->qhd', weights.astype(jnp.bfloat16), value_block, pre...  21.8 us
  transfers between devices with their start and end apart: 15, of which 8 were waited for; matrix products, arithmetic and copies ran while one was open for 14% of the time, Pallas kernels for 0%

profile of v1, /device:TPU:0, one launch (start us, length us, event | category | flops | bytes accessed | tf_op | source)
XLA Modules:
  0.0 317.8 jit_solution(10461786832355247879)
XLA Ops:
  11.1 5.0 %slice.65 = bf16[384,768]{1,0:T(8,128)(2,1)S(1)} slice(bf16[768,768]{1,0:T(8,128)(2,1)} %param.9), slice={[0:767:2], [0:768:1]} | slice | bytes 1179648 | tf_op jit(solution)/shard_map/slice | solution.py:43
  27.7 3.7 %slice.69 = bf16[384,768]{1,0:T(8,128)(2,1)} slice(bf16[772,768]{1,0:T(8,128)(2,1)S(1)} %pad_maximum_fusion), slice={[4:771:2], [0:768:1]} | slice | bytes 1179648 | tf_op jit(solution)/shard_map/slice | solution.py:43
  38.0 12.8 %psum.14 = f32[384]{0:T(512)S(1)} all-reduce(f32[384]{0:T(512)S(1)} %get-tuple-element.105), channel_id=1, replica_groups=mesh['seq'=8,'head'=4] {'head'}, use_global_device_ids=true, to_apply=%region_1.0 | all-reduce | flops 384 | bytes 3072 | tf_op jit(solution)/shard_map/psum | solution.py:27
  51.8 31.3 %all-gather.4.cloned.1.call-done = bf16[384,1536]{0,1:T(8,128)(2,1)} async-done(((bf16[384,384]{0,1:T(8,128)(2,1)}), bf16[384,1536]{0,1:T(8,128)(2,1)}) %all-gather.4.cloned.1.call-update) | async-done | bytes 1179664 | tf_op jit(solution)/shard_map/all_gather | solution.py:51
  92.3 9.9 %psum.15 = f32[384]{0:T(512)S(1)} all-reduce(f32[384]{0:T(512)S(1)} %get-tuple-element.107), channel_id=1, replica_groups=mesh['seq'=8,'head'=4] {'head'}, use_global_device_ids=true, to_apply=%region_3.0 | all-reduce | flops 384 | bytes 3072 | tf_op jit(solution)/shard_map/psum | solution.py:27
  103.0 33.5 %all-gather.6.cloned.1.call-done = bf16[384,1536]{0,1:T(8,128)(2,1)} async-done(((bf16[384,384]{0,1:T(8,128)(2,1)}), bf16[384,1536]{0,1:T(8,128)(2,1)}) %all-gather.6.cloned.1.call-update) | async-done | bytes 1179664 | tf_op jit(solution)/shard_map/all_gather | solution.py:66
  142.2 7.0 %collective-permute-done.4 = bf16[384,384]{1,0:T(8,128)(2,1)S(1)} collective-permute-done((bf16[384,384]{1,0:T(8,128)(2,1)S(1)}, bf16[384,384]{1,0:T(8,128)(2,1)S(1)}, u32[]{:S(2)}, u32[]{:S(2)}) %collective-permute-start.4) | collective-permute-done | bytes 294944 | tf_op jit(solution)/shard_map/ppermute | solution.py:87
  151.9 6.5 %collective-permute-done.5 = bf16[384,384]{1,0:T(8,128)(2,1)S(1)} collective-permute-done((bf16[384,384]{1,0:T(8,128)(2,1)S(1)}, bf16[384,384]{1,0:T(8,128)(2,1)S(1)}, u32[]{:S(2)}, u32[]{:S(2)}) %collective-permute-start.5) | collective-permute-done | bytes 294944 | tf_op jit(solution)/shard_map/ppermute | solution.py:87
  161.0 12.9 %collective-permute-done.6 = bf16[384,384]{1,0:T(8,128)(2,1)} collective-permute-done((bf16[384,384]{1,0:T(8,128)(2,1)S(1)}, bf16[384,384]{1,0:T(8,128)(2,1)}, u32[]{:S(2)}, u32[]{:S(2)}) %collective-permute-start.6) | collective-permute-done | bytes 294944 | tf_op jit(solution)/shard_map/ppermute | solution.py:87
  179.3 4.8 %collective-permute-done.7 = bf16[384,384]{1,0:T(8,128)(2,1)} collective-permute-done((bf16[384,384]{1,0:T(8,128)(2,1)}, bf16[384,384]{1,0:T(8,128)(2,1)}, u32[]{:S(2)}, u32[]{:S(2)}) %collective-permute-start.7) | collective-permute-done | bytes 294944 | tf_op jit(solution)/shard_map/ppermute | solution.py:87
  194.8 8.1 %reshape.19 = bf16[6,512,6,64]{3,2,1,0:T(8,128)(2,1)} reshape(bf16[3072,384]{1,0:T(8,128)(2,1)} %constant_dynamic-slice_fusion) | data formatting | bytes 4718592 | tf_op jit(solution)/shard_map/reshape | solution.py:96
  202.9 7.1 %copy.15 = bf16[6,512,6,64]{1,3,2,0:T(8,128)(2,1)} copy(bf16[6,512,6,64]{3,2,1,0:T(8,128)(2,1)} %reshape.19) | data formatting | bytes 4718592
  210.0 8.1 %reshape.20 = bf16[6,512,6,64]{3,2,1,0:T(8,128)(2,1)} reshape(bf16[3072,384]{1,0:T(8,128)(2,1)} %all-gather.8.cloned.1.call-done) | data formatting | bytes 4718592 | tf_op jit(solution)/shard_map/reshape | solution.py:97
  218.1 7.1 %copy.16 = bf16[6,512,6,64]{1,3,2,0:T(8,128)(2,1)} copy(bf16[6,512,6,64]{3,2,1,0:T(8,128)(2,1)} %reshape.20) | data formatting | bytes 4718592
  225.3 51.8 %while.15 = (s32[]{:T(128)}, f32[6,384]{1,0:T(8,128)S(1)}, f32[6,384]{1,0:T(8,128)S(1)}, f32[384,6,64]{0,2,1:T(8,128)S(1)}, bf16[6,512,6,64]{1,3,2,0:T(8,128)(2,...) while((s32[]{:T(128)}, f32[6,384]{1,0:T(8,128)S(1)}, ...), condition=%wide.region_7.8_spmd.clone, body=%wide.region_4.7_spmd.clone.sunk | while | flops 311883264 | bytes 35439748 | solution.py:118
  225.3 3.9 %bitcast_reduce_fusion.2 = (f32[6,384]{1,0:T(8,128)S(1)}, f32[6,512,384]{2,1,0:T(8,128)}) fusion(bf16[384,6,64]{0,2,1:T(8,128)(2,1)S(1)} %get-tuple-element.183, bf16[6,512,6,64]{1,3,2,0:T(8,128)(2,1)} %get-tuple-element.182, s32[]{:T(128)} %get-tuple-element.169), kind=kOutput, calls=%fused_computation.1.clone.1 | convolution fusion | flops 153351936 | bytes 5416448 | tf_op jit(solution)/shard_map/while/body/eval_jaxpr/qhd,khd->hqk/dot_general | solution.py:103
  233.9 3.9 %bitcast_reduce_fusion.2 = (f32[6,384]{1,0:T(8,128)S(1)}, f32[6,512,384]{2,1,0:T(8,128)}) fusion(bf16[384,6,64]{0,2,1:T(8,128)(2,1)S(1)} %get-tuple-element.183, bf16[6,512,6,64]{1,3,2,0:T(8,128)(2,1)} %get-tuple-element.182, s32[]{:T(128)} %get-tuple-element.169), kind=kOutput, calls=%fused_computation.1.clone.1 | convolution fusion | flops 153351936 | bytes 5416448 | tf_op jit(solution)/shard_map/while/body/eval_jaxpr/qhd,khd->hqk/dot_general | solution.py:103
  242.5 3.9 %bitcast_reduce_fusion.2 = (f32[6,384]{1,0:T(8,128)S(1)}, f32[6,512,384]{2,1,0:T(8,128)}) fusion(bf16[384,6,64]{0,2,1:T(8,128)(2,1)S(1)} %get-tuple-element.183, bf16[6,512,6,64]{1,3,2,0:T(8,128)(2,1)} %get-tuple-element.182, s32[]{:T(128)} %get-tuple-element.169), kind=kOutput, calls=%fused_computation.1.clone.1 | convolution fusion | flops 153351936 | bytes 5416448 | tf_op jit(solution)/shard_map/while/body/eval_jaxpr/qhd,khd->hqk/dot_general | solution.py:103
  251.2 3.9 %bitcast_reduce_fusion.2 = (f32[6,384]{1,0:T(8,128)S(1)}, f32[6,512,384]{2,1,0:T(8,128)}) fusion(bf16[384,6,64]{0,2,1:T(8,128)(2,1)S(1)} %get-tuple-element.183, bf16[6,512,6,64]{1,3,2,0:T(8,128)(2,1)} %get-tuple-element.182, s32[]{:T(128)} %get-tuple-element.169), kind=kOutput, calls=%fused_computation.1.clone.1 | convolution fusion | flops 153351936 | bytes 5416448 | tf_op jit(solution)/shard_map/while/body/eval_jaxpr/qhd,khd->hqk/dot_general | solution.py:103
  259.8 3.9 %bitcast_reduce_fusion.2 = (f32[6,384]{1,0:T(8,128)S(1)}, f32[6,512,384]{2,1,0:T(8,128)}) fusion(bf16[384,6,64]{0,2,1:T(8,128)(2,1)S(1)} %get-tuple-element.183, bf16[6,512,6,64]{1,3,2,0:T(8,128)(2,1)} %get-tuple-element.182, s32[]{:T(128)} %get-tuple-element.169), kind=kOutput, calls=%fused_computation.1.clone.1 | convolution fusion | flops 153351936 | bytes 5416448 | tf_op jit(solution)/shard_map/while/body/eval_jaxpr/qhd,khd->hqk/dot_general | solution.py:103
  263.8 3.6 %fusion.86 = f32[384,6,64]{0,2,1:T(8,128)S(1)} fusion(f32[6,512,384]{2,1,0:T(8,128)} %get-tuple-element.158, f32[6,384]{1,0:T(8,128)S(1)} %get-tuple-element.179, f32[384,6,64]{0,2,1:T(8,128)S(1)} %get-tuple-element.172, bf16[6,512,6,64]{1,3,2,0:T(8,128)(2,1)} %get-tuple-element.184, s32[]{:T(128)} %get-tuple-element.169, ...), kind=kOutput, calls=%fused_computation.9.clone.1 | convolution fusion | flops 154976256 | bytes 6310401 | tf_op jit(solution)/shard_map/while/body/eval_jaxpr/hqk,khd->qhd/dot_general | solution.py:109
  268.5 3.9 %bitcast_reduce_fusion.2 = (f32[6,384]{1,0:T(8,128)S(1)}, f32[6,512,384]{2,1,0:T(8,128)}) fusion(bf16[384,6,64]{0,2,1:T(8,128)(2,1)S(1)} %get-tuple-element.183, bf16[6,512,6,64]{1,3,2,0:T(8,128)(2,1)} %get-tuple-element.182, s32[]{:T(128)} %get-tuple-element.169), kind=kOutput, calls=%fused_computation.1.clone.1 | convolution fusion | flops 153351936 | bytes 5416448 | tf_op jit(solution)/shard_map/while/body/eval_jaxpr/qhd,khd->hqk/dot_general | solution.py:103
  272.4 3.6 %fusion.86 = f32[384,6,64]{0,2,1:T(8,128)S(1)} fusion(f32[6,512,384]{2,1,0:T(8,128)} %get-tuple-element.158, f32[6,384]{1,0:T(8,128)S(1)} %get-tuple-element.179, f32[384,6,64]{0,2,1:T(8,128)S(1)} %get-tuple-element.172, bf16[6,512,6,64]{1,3,2,0:T(8,128)(2,1)} %get-tuple-element.184, s32[]{:T(128)} %get-tuple-element.169, ...), kind=kOutput, calls=%fused_computation.9.clone.1 | convolution fusion | flops 154976256 | bytes 6310401 | tf_op jit(solution)/shard_map/while/body/eval_jaxpr/hqk,khd->qhd/dot_general | solution.py:109
  279.2 30.1 %reduce-scatter.2.cloned.1.call-done = bf16[384,384]{0,1:T(8,128)(2,1)} async-done(((bf16[384,1536]{0,1:T(8,128)(2,1)}), bf16[384,384]{0,1:T(8,128)(2,1)}) %reduce-scatter.2.cloned.1.call-update) | async-done | bytes 294928 | tf_op jit(solution)/shard_map/reduce_scatter | solution.py:126
  (130 shorter events, 85.1 us)
Async XLA Ops:
  6.5 270.6 %copy-start = (bf16[384,1536]{1,0:T(8,128)(2,1)S(1)}, bf16[384,1536]{1,0:T(8,128)(2,1)}, u32[]{:S(2)}) copy-start(bf16[384,1536]{1,0:T(8,128)(2,1)} %param.15) | copy-start | bytes 3538948
  6.5 12.0 %copy-start.2 = (bf16[768,768]{1,0:T(8,128)(2,1)S(1)}, bf16[768,768]{1,0:T(8,128)(2,1)}, u32[]{:S(2)}) copy-start(bf16[768,768]{1,0:T(8,128)(2,1)} %param.9) | copy-start | bytes 3538948
  6.5 76.6 %all-gather.4.cloned.1.call-start = ((), (), s32[]{:S(2)}) async-start(), calls=%async_computation.1 | async-start | bytes 1474560 | tf_op jit(solution)/shard_map/all_gather | solution.py:51
  7.4 14.6 %collective-permute-start = (bf16[2,768]{1,0:T(2,128)(2,1)S(1)}, bf16[2,768]{1,0:T(2,128)(2,1)S(1)}, u32[]{:S(2)}, u32[]{:S(2)}) collective-permute-start(bf16[2,768]{1,0:T(2,128)(2,1)S(1)} %get-tuple-element.103), channel_id=1, source_target_pairs={{0,4},{4,8},{8,12},{12,16},{16,20},{20,24},{24,28},{1,5},{5,9},{9,... | collective-permute-start | bytes 9224 | tf_op jit(solution)/shard_map/ppermute | solution.py:18
  9.8 12.3 %collective-permute-start.1 = (bf16[2,768]{1,0:T(2,128)(2,1)S(1)}, bf16[2,768]{1,0:T(2,128)(2,1)}, u32[]{:S(2)}, u32[]{:S(2)}) collective-permute-start(bf16[2,768]{1,0:T(2,128)(2,1)S(1)} %get-tuple-element.104), channel_id=1, source_target_pairs={{4,0},{8,4},{12,8},{16,12},{20,16},{24,20},{28,24},{5,1},{9,5},{13... | collective-permute-start | bytes 9224 | tf_op jit(solution)/shard_map/ppermute | solution.py:21
  23.0 10.0 %copy-start.3 = (f32[384,384]{0,1:T(8,128)S(1)}, f32[384,384]{0,1:T(8,128)}, u32[]{:S(2)}) copy-start(f32[384,384]{0,1:T(8,128)} %fusion.44) | copy-start | bytes 1769476
  51.8 84.7 %all-gather.6.cloned.1.call-start = ((), (), s32[]{:S(2)}) async-start(), calls=%async_computation.2 | async-start | bytes 1474560 | tf_op jit(solution)/shard_map/all_gather | solution.py:66
  83.1 6.6 %copy-start.8 = (bf16[384,1536]{0,1:T(8,128)(2,1)S(1)}, bf16[384,1536]{0,1:T(8,128)(2,1)}, u32[]{:S(2)}) copy-start(bf16[384,1536]{0,1:T(8,128)(2,1)} %all-gather.4.cloned.1.call-done) | copy-start | bytes 3538948
  83.1 6.6 %copy-start.9 = (bf16[3,384,1536]{2,1,0:T(8,128)(2,1)S(1)}, bf16[3,384,1536]{2,1,0:T(8,128)(2,1)}, u32[]{:S(2)}) copy-start(bf16[3,384,1536]{2,1,0:T(8,128)(2,1)} %param.11) | copy-start | bytes 10616836
  84.6 5.2 %collective-permute-start.2 = (bf16[4,1536]{0,1:T(8,128)(2,1)S(1)}, bf16[4,1536]{0,1:T(8,128)(2,1)S(1)}, u32[]{:S(2)}, u32[]{:S(2)}) collective-permute-start(bf16[4,1536]{0,1:T(8,128)(2,1)S(1)} %get-tuple-element.102), channel_id=1, source_target_pairs={{0,4},{4,8},{8,12},{12,16},{16,20},{20,24},{24,28},{1,5},{5,9},{9,... | collective-permute-start | bytes 36872 | tf_op jit(solution)/shard_map/ppermute | solution.py:18
  86.0 5.3 %collective-permute-start.3 = (bf16[4,1536]{0,1:T(8,128)(2,1)S(1)}, bf16[4,1536]{0,1:T(8,128)(2,1)S(1)}, u32[]{:S(2)}, u32[]{:S(2)}) collective-permute-start(bf16[4,1536]{0,1:T(8,128)(2,1)S(1)} %get-tuple-element.101), channel_id=1, source_target_pairs={{4,0},{8,4},{12,8},{16,12},{20,16},{24,20},{28,24},{5,1},{9,5},{13... | collective-permute-start | bytes 36872 | tf_op jit(solution)/shard_map/ppermute | solution.py:21
  102.9 107.1 %all-gather.8.cloned.1.call-start = ((), (), s32[]{:S(2)}) async-start(), calls=%async_computation.3 | async-start | bytes 2654208 | tf_op jit(solution)/shard_map/all_gather | solution.py:92
  139.6 169.7 %reduce-scatter.2.cloned.1.call-start = ((), (), s32[]{:S(2)}) async-start(), calls=%async_computation.4 | async-start | bytes 1474560 | tf_op jit(solution)/shard_map/reduce_scatter | solution.py:126
  142.1 7.1 %collective-permute-start.4 = (bf16[384,384]{1,0:T(8,128)(2,1)S(1)}, bf16[384,384]{1,0:T(8,128)(2,1)S(1)}, u32[]{:S(2)}, u32[]{:S(2)}) collective-permute-start(bf16[384,384]{1,0:T(8,128)(2,1)S(1)} %convolution_convert_fusion.3), channel_id=1, source_target_pairs={{0,4},{4,8},{8,12},{12,16},{16,20},{20,24},{24,28},{28,0},{1,5},{5... | collective-permute-start | bytes 884744 | tf_op jit(solution)/shard_map/ppermute | solution.py:87
  149.2 9.2 %collective-permute-start.5 = (bf16[384,384]{1,0:T(8,128)(2,1)S(1)}, bf16[384,384]{1,0:T(8,128)(2,1)S(1)}, u32[]{:S(2)}, u32[]{:S(2)}) collective-permute-start(bf16[384,384]{1,0:T(8,128)(2,1)S(1)} %collective-permute-done.4), channel_id=1, source_target_pairs={{0,4},{4,8},{8,12},{12,16},{16,20},{20,24},{24,28},{28,0},{1,5},{5... | collective-permute-start | bytes 884744 | tf_op jit(solution)/shard_map/ppermute | solution.py:87
  149.2 9.2 %collective-permute-start.8 = (bf16[384,384]{1,0:T(8,128)(2,1)S(1)}, bf16[384,384]{1,0:T(8,128)(2,1)}, u32[]{:S(2)}, u32[]{:S(2)}) collective-permute-start(bf16[384,384]{1,0:T(8,128)(2,1)S(1)} %convolution_convert_fusion.3), channel_id=1, source_target_pairs={{0,28},{4,0},{8,4},{12,8},{16,12},{20,16},{24,20},{28,24},{1,29},{... | collective-permute-start | bytes 884744 | tf_op jit(solution)/shard_map/ppermute | solution.py:89
  158.4 15.6 %collective-permute-start.6 = (bf16[384,384]{1,0:T(8,128)(2,1)S(1)}, bf16[384,384]{1,0:T(8,128)(2,1)}, u32[]{:S(2)}, u32[]{:S(2)}) collective-permute-start(bf16[384,384]{1,0:T(8,128)(2,1)S(1)} %collective-permute-done.5), channel_id=1, source_target_pairs={{0,4},{4,8},{8,12},{12,16},{16,20},{20,24},{24,28},{28,0},{1,5},{5... | collective-permute-start | bytes 884744 | tf_op jit(solution)/shard_map/ppermute | solution.py:87
  159.1 17.3 %collective-permute-start.9 = (bf16[384,384]{1,0:T(8,128)(2,1)}, bf16[384,384]{1,0:T(8,128)(2,1)}, u32[]{:S(2)}, u32[]{:S(2)}) collective-permute-start(bf16[384,384]{1,0:T(8,128)(2,1)} %collective-permute-done.8), channel_id=1, source_target_pairs={{0,28},{4,0},{8,4},{12,8},{16,12},{20,16},{24,20},{28,24},{1,29},{... | collective-permute-start | bytes 884744 | tf_op jit(solution)/shard_map/ppermute | solution.py:89
  174.0 10.2 %collective-permute-start.7 = (bf16[384,384]{1,0:T(8,128)(2,1)}, bf16[384,384]{1,0:T(8,128)(2,1)}, u32[]{:S(2)}, u32[]{:S(2)}) collective-permute-start(bf16[384,384]{1,0:T(8,128)(2,1)} %collective-permute-done.6), channel_id=1, source_target_pairs={{0,4},{4,8},{8,12},{12,16},{16,20},{20,24},{24,28},{28,0},{1,5},{5... | collective-permute-start | bytes 884744 | tf_op jit(solution)/shard_map/ppermute | solution.py:87
  174.0 12.2 %copy-start.7 = (bf16[384,384]{1,0:T(8,128)(2,1)S(1)}, bf16[384,384]{1,0:T(8,128)(2,1)}, u32[]{:S(2)}) copy-start(bf16[384,384]{1,0:T(8,128)(2,1)} %copy-done.6) | copy-start | bytes 884740
  176.4 11.9 %collective-permute-start.10 = (bf16[384,384]{1,0:T(8,128)(2,1)}, bf16[384,384]{1,0:T(8,128)(2,1)S(1)}, u32[]{:S(2)}, u32[]{:S(2)}) collective-permute-start(bf16[384,384]{1,0:T(8,128)(2,1)} %collective-permute-done.9), channel_id=1, source_target_pairs={{0,28},{4,0},{8,4},{12,8},{16,12},{20,16},{24,20},{28,24},{1,29},{... | collective-permute-start | bytes 884744 | tf_op jit(solution)/shard_map/ppermute | solution.py:89
  229.2 3.9 %copy-start.1 = (f32[6,512,384]{2,1,0:T(8,128)S(1)}, f32[6,512,384]{2,1,0:T(8,128)}, u32[]{:S(2)}) copy-start(f32[6,512,384]{2,1,0:T(8,128)} %get-tuple-element.158) | copy-start | bytes 14155780 | tf_op jit(solution)/shard_map/while
  237.9 3.9 %copy-start.1 = (f32[6,512,384]{2,1,0:T(8,128)S(1)}, f32[6,512,384]{2,1,0:T(8,128)}, u32[]{:S(2)}) copy-start(f32[6,512,384]{2,1,0:T(8,128)} %get-tuple-element.158) | copy-start | bytes 14155780 | tf_op jit(solution)/shard_map/while
  246.5 3.9 %copy-start.1 = (f32[6,512,384]{2,1,0:T(8,128)S(1)}, f32[6,512,384]{2,1,0:T(8,128)}, u32[]{:S(2)}) copy-start(f32[6,512,384]{2,1,0:T(8,128)} %get-tuple-element.158) | copy-start | bytes 14155780 | tf_op jit(solution)/shard_map/while
  (6 other events, 19.1 us)
Sparse Core Ops, SparseCore 0:
  51.9 31.1 all-gather.3
  103.0 33.3 all-gather.5
  139.7 35.6 all-gather.7
  279.3 29.9 reduce-scatter.1
